TPU v7x, 512 devices: a whole 4x4x16 slice. The times are simulated.
512 devices in a mesh: tm: 32 (over z, core), row: 16 (over x, y).
Axes of the slice: x: 4, y: 4, z: 16, core: 2. Of those that a mesh axis runs over, the one named last changes fastest.
Arguments:
- video: bfloat16 [32, 4, 384, 1024], P('tm', None, 'row'), may hold values from -6 to 6
- stem_weight: bfloat16 [64, 4, 3, 3], replicated, may hold values from -1 to 1
- w_qkv: bfloat16 [1536, 2304], P('tm'), may hold values from -0.15625 to 0.15625
- decay: float32 [32, 6], P('tm'), may hold values from 0.04 to 1, as said below
Outputs:
- mixed: bfloat16 [32, 32, 128, 768], P('tm', 'row')
Inputs may be any that keep to these rules, and one draw needn't show every extreme that they name: decay lies in (0, 1].
All inputs are finite; a program needn't handle non-finite values.
Results may differ from a plain program's by a relative error of at most 0.012.
Values may be sent and summed in bfloat16 or wider, within the bound.
A program may use at most 128 MiB of HBM per device.

v0:
```python
import jax
import jax.numpy as jnp
from jax import lax
from jax.sharding import PartitionSpec as P

HEADS = 6


def shifted(block, axis, distance):
    devices = range(lax.axis_size(axis))
    route = [(i - distance, i) for i in devices if i - distance in devices]
    return lax.ppermute(block, axis, route)


def prefix_2(x, axis, join, neutral):
    place = lax.axis_index(axis)
    gathered = jax.tree.map(
        lambda a, kind: lax.all_gather(a.astype(kind), axis), x, (jnp.bfloat16, jnp.bfloat16)
    )
    state = jax.tree.map(lambda a, e: jnp.zeros_like(a) + jnp.asarray(e, a.dtype), x, neutral)

    def one(step, state):
        return join(
            state,
            jax.tree.map(
                lambda a, own: lax.dynamic_index_in_dim(a, step, 0, False).astype(own.dtype),
                gathered,
                x,
            ),
        )

    return lax.fori_loop(0, place, one, state)


def combine(first_pair, later_pair):
    return (first_pair[0] * later_pair[0], later_pair[0] * first_pair[1] + later_pair[1])


def summarize(frame_rates, outer_sums):
    factor = jnp.ones_like(frame_rates[0])
    summed = jnp.zeros_like(outer_sums[0])
    factor = factor * frame_rates[0]
    summed = frame_rates[0] * summed + outer_sums[0]
    return (factor, summed)


def unroll(prefix, frame_rates, outer_sums):
    running = prefix
    running = frame_rates[0] * running + outer_sums[0]
    collected = [running]
    return jnp.stack(collected, axis=0)


def local(video, stem_weight, w_qkv, decay):
    frames_dev = video.shape[0]
    upper_row = shifted(video[:, :, -1:, :], "row", 1)
    padded = jnp.concatenate([upper_row, video], axis=2)
    padded = jnp.pad(padded, ((0, 0), (0, 0), (0, 0), (1, 0)))
    stem_out = lax.conv_general_dilated(
        padded,
        stem_weight,
        (2, 2),
        "VALID",
        dimension_numbers=("NCHW", "OIHW", "NCHW"),
        preferred_element_type=jnp.float32,
    )
    features = jnp.tanh(stem_out).astype(jnp.bfloat16)
    channels = features.shape[1]
    patch_rows = features.shape[2] // 6
    patch_cols = features.shape[3] // 4
    frame_tokens = patch_rows * patch_cols
    shaped = features.reshape(frames_dev, channels, patch_rows, 6, patch_cols, 4).transpose(
        0, 2, 4, 1, 3, 5
    )
    tokens = shaped.reshape(frames_dev * frame_tokens, channels * 24)
    qkv_width = w_qkv.shape[1]
    empty = jnp.zeros((tokens.shape[0], qkv_width), jnp.float32)
    block_rows = lax.all_gather(w_qkv, "tm", axis=0, tiled=True)
    columns = lax.slice_in_dim(tokens, 0, block_rows.shape[0], axis=1)
    projected = (empty + jnp.dot(columns, block_rows, preferred_element_type=jnp.float32)).astype(
        jnp.bfloat16
    )
    inner_width = qkv_width // 3
    head_size = inner_width // HEADS
    queries = projected[:, :inner_width].reshape(frames_dev, frame_tokens, HEADS, head_size)
    keys = projected[:, inner_width : 2 * inner_width].reshape(
        frames_dev, frame_tokens, HEADS, head_size
    )
    values = projected[:, 2 * inner_width :].reshape(frames_dev, frame_tokens, HEADS, head_size)
    kv_local = jnp.einsum("fnhd,fnhe->fhde", keys, values, preferred_element_type=jnp.float32)
    head_rates = decay[:, :, None, None]
    kv_total = lax.psum(kv_local.astype(jnp.bfloat16), "row").astype(jnp.float32)
    factor, summed = summarize(head_rates, kv_total)
    prefix = prefix_2(
        (factor, summed), "tm", combine, (jnp.ones_like(factor), jnp.zeros_like(summed))
    )[1]
    states = unroll(prefix, head_rates, kv_total).astype(jnp.bfloat16)
    attended = jnp.einsum("fnhd,fhde->fnhe", queries, states, preferred_element_type=jnp.float32)
    attended = attended * lax.rsqrt(jnp.mean(attended * attended, axis=-1, keepdims=True) + 1e-06)
    return attended.reshape(frames_dev, patch_rows, patch_cols, inner_width).astype(jnp.bfloat16)


def solution(mesh):
    return jax.shard_map(
        local,
        mesh=mesh,
        in_specs=(P("tm", None, "row", None), P(), P("tm", None), P("tm", None)),
        out_specs=P("tm", "row", None, None),
        check_vma=False,
    )
```

profile of v0, /device:TPU:491, one launch (start us, length us, event | category | flops | bytes accessed | tf_op | source)
XLA Modules:
  0.0 324.3 jit_solution(5156422705934072437)
XLA Ops:
  8.2 3.2 collective-permute-start
  11.4 1.3 collective-permute-done
  13.8 1.3 reshape.102
  15.1 4.3 %copy.74 = bf16[4,25,1,8,130]{3,0,4,1,2:T(4,128)(2,1)S(1)} copy(bf16[4,25,1,8,130]{4,3,1,0,2:T(8,128)(2,1)} %reshape.102) | data formatting | bytes 416000 | tf_op jit(solution)/shard_map/conv_general_dilated | solution.py:59
  19.6 5.0 %fusion.3 = f32[12,8,65,64]{3,1,2,0:T(8,128)} fusion(bf16[64,4,3,3]{0,1,3,2:T(4,128)(2,1)S(1)} %copy-done, bf16[4,25,1,7,2]{3,0,4,1,2:T(4,128)(2,1)S(1)} %slice.18, bf16[4,25,1,8,130]{3,0,4,1,2:T(4,128)(2,1)S(1)} %copy.74), kind=kOutput, calls=%fused_computation.7 | convolution fusion | flops 29387520 | bytes 1812848 | tf_op jit(solution)/shard_map/conv_general_dilated | solution.py:59
  24.5 3.4 %copy.75 = f32[12,8,65,64]{2,3,1,0:T(8,128)S(1)} copy(f32[12,8,65,64]{3,1,2,0:T(8,128)} %fusion.3) | data formatting | bytes 3194880 | tf_op jit(solution)/shard_map/conv_general_dilated | solution.py:59
  28.4 1.2 copy.76
  29.6 1.2 reshape.91
  31.8 1.3 copy.78
  33.0 52.2 %all-gather.5.cloned.1.call-done = bf16[1536,2304]{1,0:T(8,128)(2,1)} async-done(((bf16[48,2304]{1,0:T(8,128)(2,1)}), bf16[1536,2304]{1,0:T(8,128)(2,1)}) %all-gather.5.cloned.1.call-update) | async-done | bytes 7077904 | tf_op jit(solution)/shard_map/all_gather | solution.py:78
  85.2 5.0 %convolution_convert_fusion = bf16[256,2304]{1,0:T(8,128)(2,1)S(1)} fusion(bf16[1536,2304]{1,0:T(8,128)(2,1)} %all-gather.5.cloned.1.call-done, bf16[192,8,2,128]{3,2,1,0:T(2,128)(2,1)S(1)} %bitcast.66), kind=kOutput, calls=%fused_computation.4 | convolution fusion | flops 1812529152 | bytes 9043968 | tf_op jit(solution)/shard_map/dot_general | solution.py:80
  91.7 108.5 %all-reduce.2.cloned.1.call-done = bf16[1,6,128,128]{3,2,1,0:T(8,128)(2,1)} async-done(((bf16[1,6,128,128]{3,2,1,0:T(8,128)(2,1)}), bf16[1,6,128,128]{3,2,1,0:T(8,128)(2,1)}) %all-reduce.2.cloned.1.call-update) | async-done | bytes 196624 | tf_op jit(solution)/shard_map/psum | solution.py:92
  200.3 1.7 fusion.9
  202.0 30.6 %all-gather.1 = bf16[32,1,6]{2,1,0:T(2,128)(2,1)S(1)} all-gather(bf16[1,1,6]{2,1,0:T(2,128)(2,1)S(1)} %convert_bitcast_fusion.1), channel_id=2, replica_groups=mesh['tm'=32,'row'=16] {'tm'}, dimensions={0}, use_global_device_ids=true | all-gather | bytes 396 | tf_op jit(solution)/shard_map/all_gather | solution.py:18
  233.0 48.6 %all-gather.7.cloned.1.call-done = bf16[32,6,128,128]{3,2,1,0:T(8,128)(2,1)} async-done(((bf16[1,6,128,128]{3,2,1,0:T(8,128)(2,1)}), bf16[32,6,128,128]{3,2,1,0:T(8,128)(2,1)}) %all-gather.7.cloned.1.call-update) | async-done | bytes 6291472 | tf_op jit(solution)/shard_map/all_gather | solution.py:18
  281.7 34.4 %while.12 = (s32[]{:T(128)}, f32[6,128,128]{2,1,0:T(8,128)S(1)}, s32[]{:T(128)}, bf16[32,6,1,1]{1,3,2,0:T(2,128)(2,1)S(1)}, bf16[32,6,128,128]{3,2,1,0:T(8,128)(2,1)}, /*index=5*/s32[]{:T(128)}, s32[]{:T(128)}, s32[]{:T(128)}) while((s32[]{:T(128)}, f32[6,128,128]{2,1,0:T(8,128)S(1)}, s32[]{:T(128)}, bf16[32,6,1,1]{1,3,2,0:T(2,128)(2,1)S(1)}, ...), condition=%wide.region_2.3_spmd, body=%wide.region_1.2_spmd.sunk | while | flops 294923 | bytes 983227 | solution.py:32
  281.7 1.1 convert_add_fusion.3
  284.0 1.1 convert_add_fusion.3
  285.1 1.1 convert_add_fusion.3
  288.4 1.1 convert_add_fusion.3
  291.7 1.1 convert_add_fusion.3
  295.1 1.1 convert_add_fusion.3
  298.4 1.1 convert_add_fusion.3
  301.7 1.1 convert_add_fusion.3
  (90 shorter events, 32.5 us)
Async XLA Ops:
  6.5 13.0 %copy-start = (bf16[64,4,3,3]{0,1,3,2:T(4,128)(2,1)S(1)}, bf16[64,4,3,3]{0,1,3,2:T(4,128)(2,1)}, u32[]{:S(2)}) copy-start(bf16[64,4,3,3]{0,1,3,2:T(4,128)(2,1)} %param.7) | copy-start | bytes 13828
  6.5 78.7 %all-gather.5.cloned.1.call-start = ((), (), s32[]{:S(2)}) async-start(), calls=%async_computation | async-start | bytes 7299072 | tf_op jit(solution)/shard_map/all_gather | solution.py:78
  7.3 193.0 %all-reduce.2.cloned.1.call-start = ((), (), s32[]{:S(2)}) async-start(), calls=%async_computation.1 | async-start | bytes 393216 | tf_op jit(solution)/shard_map/psum | solution.py:92
  8.2 4.5 %collective-permute-start = (bf16[1,4,1,1024]{3,2,1,0:T(2,128)(2,1)S(1)}, bf16[1,4,1,1024]{3,2,1,0:T(2,128)(2,1)S(1)}, u32[]{:S(2)}, u32[]{:S(2)}) collective-permute-start(bf16[1,4,1,1024]{3,2,1,0:T(2,128)(2,1)S(1)} %slice.12), channel_id=1, source_target_pairs={{0,1},{1,2},{2,3},{3,4},{4,5},{5,6},{6,7},{7,8},{8,9},{9,10},{10,1... | collective-permute-start | bytes 24584 | tf_op jit(solution)/shard_map/ppermute | solution.py:12
  24.5 3.4 %copy-start.2 = (pred[8,65]{1,0:T(8,128)(4,1)S(1)}, pred[8,65]{1,0:T(8,128)(4,1)}, u32[]{:S(2)}) copy-start(pred[8,65]{1,0:T(8,128)(4,1)} %constant.40) | copy-start | bytes 1564
  90.3 1.5 copy-start.3
  91.7 190.0 %all-gather.7.cloned.1.call-start = ((), (), s32[]{:S(2)}) async-start(), calls=%async_computation.2 | async-start | bytes 6488064 | tf_op jit(solution)/shard_map/all_gather | solution.py:18
  202.0 114.2 %copy-start.1 = (bf16[1,6,128,128]{3,2,1,0:T(8,128)(2,1)S(1)}, bf16[1,6,128,128]{3,2,1,0:T(8,128)(2,1)}, u32[]{:S(2)}) copy-start(bf16[1,6,128,128]{3,2,1,0:T(8,128)(2,1)} %all-reduce.2.cloned.1.call-done) | copy-start | bytes 589828
Sparse Core Ops, SparseCore 0:
  9.5 75.6 all-gather.4
  91.8 108.4 all-reduce.1
  202.4 79.2 all-gather.6
where the time goes:
time: 326 us; the launch traced here: 324 us
  waiting for transfers between devices  211 us (65%)
  other arithmetic  36.6 us (11%)
  blocking collectives  30.6 us (9%)
  local copies, waits for them, and re-layouts  16.7 us (5%)
  between operations  13.3 us (4%)
  matrix products  11.4 us (3%)
  starting transfers between devices  3.29 us (1%)
    psum x1, waiting for transfers between devices, local(): lax.psum(kv_local.astype(jnp.bfloat16), 'row').astype(jnp.float32)  109 us
    all_gather x1, waiting for transfers between devices, local(): block_rows = lax.all_gather(w_qkv, 'tm', axis=0, tiled=True)  52.2 us
    all_gather x1, waiting for transfers between devices, prefix_2(): lax.all_gather(a.astype(kind), axis)  48.6 us
    add x31, other arithmetic, combine(): later_pair[0] * first_pair[1] + later_pair[1]  33.1 us
    all_gather x1, blocking collectives, prefix_2(): lax.all_gather(a.astype(kind), axis)  30.6 us
    conv_general_dilated x4, local copies, waits for them, and re-layouts, local(): lax.conv_general_dilated(padded, stem_weight, (2, 2), 'VALID', dimension_...  9.06 us
  transfers between devices with their start and end apart: 4, of which 4 were waited for; matrix products, arithmetic and copies ran while one was open for 7% of the time, Pallas kernels for 0%

commit v1 on v0

--- a/solution.py
+++ b/solution.py
@@ -75,7 +75,9 @@
     tokens = shaped.reshape(frames_dev * frame_tokens, channels * 24)
     qkv_width = w_qkv.shape[1]
     empty = jnp.zeros((tokens.shape[0], qkv_width), jnp.float32)
-    block_rows = lax.all_gather(w_qkv, "tm", axis=0, tiled=True)
+    block_rows = jnp.concatenate(
+        lax.all_to_all(jnp.stack([w_qkv] * lax.axis_size("tm")), "tm", 0, 0), axis=0
+    )
     columns = lax.slice_in_dim(tokens, 0, block_rows.shape[0], axis=1)
     projected = (empty + jnp.dot(columns, block_rows, preferred_element_type=jnp.float32)).astype(
         jnp.bfloat16

time: 326 us -> 570 us (1.75)
  the two profiles are of different devices: /device:TPU:491 before, /device:TPU:485 now
where the time goes in v1:
time: 570 us; the launch traced here: 569 us
  waiting for transfers between devices  444 us (78%)
  other arithmetic  35.7 us (6%)
  blocking collectives  30.8 us (5%)
  local copies, waits for them, and re-layouts  20.1 us (4%)
  between operations  13.6 us (2%)
  starting transfers between devices  12.9 us (2%)
  matrix products  11.3 us (2%)
    all_to_all x1, waiting for transfers between devices, local(): lax.all_to_all(jnp.stack([w_qkv] * lax.axis_size('tm')), 'tm', 0, 0)  274 us
    psum x1, waiting for transfers between devices, local(): lax.psum(kv_local.astype(jnp.bfloat16), 'row').astype(jnp.float32)  119 us
    all_gather x1, waiting for transfers between devices, prefix_2(): lax.all_gather(a.astype(kind), axis)  48 us
    add x31, other arithmetic, combine(): later_pair[0] * first_pair[1] + later_pair[1]  33.1 us
    all_gather x1, blocking collectives, prefix_2(): lax.all_gather(a.astype(kind), axis)  30.8 us
  transfers between devices with their start and end apart: 4, of which 4 were waited for; matrix products, arithmetic and copies ran while one was open for 3% of the time, Pallas kernels for 0%

profile of v1, /device:TPU:485, one launch (start us, length us, event | category | flops | bytes accessed | tf_op | source)
XLA Modules:
  0.0 569.2 jit_solution(3549427136015320391)
XLA Ops:
  6.5 4.3 stack.2
  10.9 9.6 %all-to-all-start = ((bf16[32,48,2304]{2,1,0:T(8,128)(2,1)}), bf16[32,48,2304]{2,1,0:T(8,128)(2,1)}, u32[]{:S(2)}, u32[]{:S(2)}) async-start(bf16[32,48,2304]{2,1,0:T(8,128)(2,1)} %stack.2), calls=%async_computation | async-start | bytes 14155776 | tf_op jit(solution)/shard_map/all_to_all | solution.py:79
  20.5 3.2 collective-permute-start
  23.7 3.4 collective-permute-done
  27.3 1.3 reshape.108
  28.7 4.3 copy.74
  33.1 4.9 fusion.3
  38.0 3.3 copy.75
  41.7 1.2 copy.76
  43.0 1.2 reshape.97
  45.1 1.3 copy.78
  46.4 273.6 %all-to-all-done = bf16[32,48,2304]{2,1,0:T(8,128)(2,1)} async-done(((bf16[32,48,2304]{2,1,0:T(8,128)(2,1)}), bf16[32,48,2304]{2,1,0:T(8,128)(2,1)}, u32[]{:S(2)}, u32[]{:S(2)}) %all-to-all-start) | async-done | bytes 7077920 | tf_op jit(solution)/shard_map/all_to_all | solution.py:79
  319.9 5.0 convolution_convert_fusion
  326.5 118.9 %all-reduce.2.cloned.1.call-done = bf16[1,6,128,128]{3,2,1,0:T(8,128)(2,1)} async-done(((bf16[1,6,128,128]{3,2,1,0:T(8,128)(2,1)}), bf16[1,6,128,128]{3,2,1,0:T(8,128)(2,1)}) %all-reduce.2.cloned.1.call-update) | async-done | bytes 196624 | tf_op jit(solution)/shard_map/psum | solution.py:94
  445.4 1.7 fusion.9
  447.2 30.8 %all-gather.1 = bf16[32,1,6]{2,1,0:T(2,128)(2,1)S(1)} all-gather(bf16[1,1,6]{2,1,0:T(2,128)(2,1)S(1)} %convert_bitcast_fusion.1), channel_id=2, replica_groups=mesh['tm'=32,'row'=16] {'tm'}, dimensions={0}, use_global_device_ids=true | all-gather | bytes 396 | tf_op jit(solution)/shard_map/all_gather | solution.py:18
  478.3 48.0 %all-gather.4.cloned.1.call-done = bf16[32,6,128,128]{3,2,1,0:T(8,128)(2,1)} async-done(((bf16[1,6,128,128]{3,2,1,0:T(8,128)(2,1)}), bf16[32,6,128,128]{3,2,1,0:T(8,128)(2,1)}) %all-gather.4.cloned.1.call-update) | async-done | bytes 6291472 | tf_op jit(solution)/shard_map/all_gather | solution.py:18
  526.4 34.3 %while.12 = (s32[]{:T(128)}, f32[6,128,128]{2,1,0:T(8,128)S(1)}, s32[]{:T(128)}, bf16[32,6,1,1]{1,3,2,0:T(2,128)(2,1)S(1)}, bf16[32,6,128,128]{3,2,1,0:T(8,128)(2,1)}, /*index=5*/s32[]{:T(128)}, s32[]{:T(128)}, s32[]{:T(128)}) while((s32[]{:T(128)}, f32[6,128,128]{2,1,0:T(8,128)S(1)}, s32[]{:T(128)}, bf16[32,6,1,1]{1,3,2,0:T(2,128)(2,1)S(1)}, ...), condition=%wide.region_2.3_spmd, body=%wide.region_1.2_spmd.sunk | while | flops 294923 | bytes 983235 | solution.py:32
  529.7 1.1 convert_add_fusion.3
  530.8 1.1 convert_add_fusion.3
  531.9 1.1 convert_add_fusion.3
  536.4 1.1 convert_add_fusion.3
  537.5 1.1 convert_add_fusion.3
  538.6 1.1 convert_add_fusion.3
  (92 shorter events, 32.2 us)
Async XLA Ops:
  6.5 26.5 %copy-start = (bf16[64,4,3,3]{0,1,3,2:T(4,128)(2,1)S(1)}, bf16[64,4,3,3]{0,1,3,2:T(4,128)(2,1)}, u32[]{:S(2)}) copy-start(bf16[64,4,3,3]{0,1,3,2:T(4,128)(2,1)} %param.7) | copy-start | bytes 13828
  10.9 9.6 %copy-start.2 = (bf16[1,4,24,1024]{3,2,1,0:T(8,128)(2,1)S(1)}, bf16[1,4,24,1024]{3,2,1,0:T(8,128)(2,1)}, u32[]{:S(2)}) copy-start(bf16[1,4,24,1024]{3,2,1,0:T(8,128)(2,1)} %param.6) | copy-start | bytes 589828
  10.9 309.1 %all-to-all-start = ((bf16[32,48,2304]{2,1,0:T(8,128)(2,1)}), bf16[32,48,2304]{2,1,0:T(8,128)(2,1)}, u32[]{:S(2)}, u32[]{:S(2)}) async-start(bf16[32,48,2304]{2,1,0:T(8,128)(2,1)} %stack.2), calls=%async_computation | async-start | bytes 14155776 | tf_op jit(solution)/shard_map/all_to_all | solution.py:79
  20.4 425.0 %all-reduce.2.cloned.1.call-start = ((), (), s32[]{:S(2)}) async-start(), calls=%async_computation.1 | async-start | bytes 393216 | tf_op jit(solution)/shard_map/psum | solution.py:94
  20.5 6.6 %collective-permute-start = (bf16[1,4,1,1024]{3,2,1,0:T(2,128)(2,1)S(1)}, bf16[1,4,1,1024]{3,2,1,0:T(2,128)(2,1)S(1)}, u32[]{:S(2)}, u32[]{:S(2)}) collective-permute-start(bf16[1,4,1,1024]{3,2,1,0:T(2,128)(2,1)S(1)} %slice.12), channel_id=1, source_target_pairs={{0,1},{1,2},{2,3},{3,4},{4,5},{5,6},{6,7},{7,8},{8,9},{9,10},{10,1... | collective-permute-start | bytes 24584 | tf_op jit(solution)/shard_map/ppermute | solution.py:12
  38.0 3.3 copy-start.3
  325.0 1.5 copy-start.4
  326.4 199.9 %all-gather.4.cloned.1.call-start = ((), (), s32[]{:S(2)}) async-start(), calls=%async_computation.2 | async-start | bytes 6488064 | tf_op jit(solution)/shard_map/all_gather | solution.py:18
  447.1 113.5 %copy-start.1 = (bf16[1,6,128,128]{3,2,1,0:T(8,128)(2,1)S(1)}, bf16[1,6,128,128]{3,2,1,0:T(8,128)(2,1)}, u32[]{:S(2)}) copy-start(bf16[1,6,128,128]{3,2,1,0:T(8,128)(2,1)} %all-reduce.2.cloned.1.call-done) | copy-start | bytes 589828
Sparse Core Ops, SparseCore 0:
  326.5 118.8 all-reduce.1
  447.5 78.7 all-gather.3
